TPU v7x, 256 devices: a whole 4x4x8 slice. The times are simulated.
256 devices in a mesh: rows: 32 (over z, x), far: 8 (over y, core).
Axes of the slice: x: 4, y: 4, z: 8, core: 2. Of those that a mesh axis runs over, the one named last changes fastest.
Arguments:
- right_side: float32 [65536, 256], P('rows'), may hold values from -24 to 24
- near_blocks: float32 [512, 48, 128, 128], P('rows', 'far'), may hold values from -0.0234375 to 0.0234375
- near_cols: int32 [512, 48], P('rows', 'far'), may hold values from 0 to 511, as said below
- far_src: int32 [32, 32, 8], P('rows', None, 'far'), may hold values from 0 to 15
- far_tgt: int32 [32, 32, 8], P('rows', None, 'far'), may hold values from 0 to 15
- far_left: float32 [32, 32, 8, 128, 64], P('rows', None, 'far'), may hold values from -0.0546875 to 0.0546875
- far_right: float32 [32, 32, 8, 128, 64], P('rows', None, 'far'), may hold values from -0.5 to 0.5
Outputs:
- solution: float32 [65536, 256], P('rows', 'far')
- residual: float32 [65536, 256], P('rows', 'far')
Inputs may be any that keep to these rules, and one draw needn't show every extreme that they name: `near_cols`: each near-field column lies within 8 clusters of its row; slot 0 of row i names i itself, slot 1 names min(i + 8, 511) and slot 2 names max(i - 8, 0).
All inputs are finite; a program needn't handle non-finite values.
Results may differ from a plain program's by a relative error of at most 0.0003.
Values sent between devices are 32-bit elements; how exact they have to be, the bound alone decides.
A program may use at most 128 MiB of HBM per device.

v0:
```python
import jax
import jax.numpy as jnp
from jax import lax
from jax.sharding import PartitionSpec as P

B = 128
CL_DEV = 16
REACH = 8
TOP_PRECISION = lax.Precision.HIGHEST
EPS = 1e-06


def with_halo(cells, sides, width):
    for axis, dim in sides:
        count = lax.axis_size(axis)
        ends = count - 1
        head = lax.slice_in_dim(cells, 0, width, axis=dim)
        tail = lax.slice_in_dim(cells, cells.shape[dim] - width, cells.shape[dim], axis=dim)
        cells = jnp.concatenate(
            [
                lax.ppermute(tail, axis, [(i, (i + 1) % count) for i in range(ends)]),
                cells,
                lax.ppermute(head, axis, [((i + 1) % count, i) for i in range(ends)]),
            ],
            axis=dim,
        )
    return cells


def column_dots(left_vec, right_vector):
    return jnp.sum(left_vec * right_vector, axis=0)


def near_term(vector_in, near_blocks, near_cols):
    rhs_count = vector_in.shape[1]
    padded = with_halo(vector_in, (("rows", 0),), REACH * B)
    clusters = padded.reshape(-1, B, rhs_count)
    offset = lax.axis_index("rows") * CL_DEV - REACH
    picked = jnp.take(clusters, near_cols - offset, axis=0)
    return jnp.einsum("cspq,csqn->cpn", near_blocks, picked, precision=TOP_PRECISION)


def far_term(vector_in, far_src, far_tgt, far_left, far_right):
    clusters = vector_in.reshape(CL_DEV, B, vector_in.shape[1])
    picked = jnp.take(clusters, far_src[0], axis=0)
    coefficients = jnp.einsum("tsbr,tsbn->tsrn", far_right[0], picked, precision=TOP_PRECISION)
    owning_devices = (far_tgt[0][:, :, None] == jnp.arange(CL_DEV, dtype=jnp.int32)).astype(
        jnp.float32
    )
    contribution_part = jnp.einsum(
        "asbr,asrn->asbn",
        far_left[0],
        lax.all_to_all(coefficients, "rows", split_axis=0, concat_axis=0, tiled=True),
        precision=TOP_PRECISION,
    )
    return jnp.einsum("hyo,hyze->oze", owning_devices, contribution_part, precision=TOP_PRECISION)


def own_columns(vector_in):
    share_width = vector_in.shape[-1] // lax.axis_size("far")
    return lax.dynamic_slice_in_dim(
        vector_in, lax.axis_index("far") * share_width, share_width, vector_in.ndim - 1
    )


def least_squares(rhs_length, upper_left, lower_left, column_two, lower_right):
    radius_one = jnp.sqrt(upper_left * upper_left + lower_left * lower_left)
    cosine_one = upper_left / radius_one
    sine_one = lower_left / radius_one
    rotated_top = cosine_one * rhs_length
    rotated_mid = -sine_one * rhs_length
    coupled = cosine_one * column_two[0] + sine_one * column_two[1]
    diagonal_two = cosine_one * column_two[1] - sine_one * column_two[0]
    radius_two = jnp.sqrt(diagonal_two * diagonal_two + lower_right * lower_right)
    weight_two = diagonal_two * rotated_mid / (radius_two * radius_two)
    weight_one = (rotated_top - coupled * weight_two) / radius_one
    return (weight_one, weight_two)


def shards(right_side, near_blocks, near_cols, far_src, far_tgt, far_left, far_right):

    def partial_image(vector_in):
        near_part = near_term(vector_in, near_blocks, near_cols)
        far_part = far_term(vector_in, far_src, far_tgt, far_left, far_right)
        return (near_part + far_part).reshape(vector_in.shape)

    def finish(vector_in):
        return own_columns(vector_in)

    def apply_op(vector_in):
        return 0.5 * vector_in + lax.psum(partial_image(vector_in), "far")

    def orthogonal(vectors, candidate):
        heights = lax.psum(jnp.stack([column_dots(item, candidate) for item in vectors]), "rows")
        for slot_id in range(len(vectors)):
            candidate = candidate - heights[slot_id] * vectors[slot_id]
        length = jnp.sqrt(lax.psum(column_dots(candidate, candidate), "rows") + EPS)
        return (heights, candidate, length)

    rhs_length = jnp.sqrt(lax.psum(column_dots(right_side, right_side), "rows") + EPS)
    first_full = right_side / rhs_length
    image_one = apply_op(first_full)
    heights_one, candidate, lower_left = orthogonal((first_full,), image_one)
    second_vec = candidate / lower_left
    image_two = apply_op(second_vec)
    heights_two, candidate, lower_right = orthogonal((first_full, second_vec), image_two)
    weight_one, weight_two = least_squares(
        rhs_length, heights_one[0], lower_left, heights_two, lower_right
    )
    own_solution = weight_one * first_full + weight_two * second_vec
    own_residual = right_side - weight_one * image_one - weight_two * image_two
    return (finish(own_solution), finish(own_residual))


def solution(mesh):
    return jax.shard_map(
        shards,
        mesh=mesh,
        in_specs=(
            P("rows", None),
            P("rows", "far", None, None),
            P("rows", "far"),
            P("rows", None, "far"),
            P("rows", None, "far"),
            P("rows", None, "far", None, None),
            P("rows", None, "far", None, None),
        ),
        out_specs=(P("rows", "far"), P("rows", "far")),
        check_vma=False,
    )
```

profile of v0, /device:TPU:2, one launch (start us, length us, event | category | flops | bytes accessed | tf_op | source)
XLA Modules:
  0.0 811.1 jit_solution(4049094716238253556)
XLA Ops:
  8.6 1.9 multiply_reduce_fusion.5
  10.5 1.9 copy.35
  12.4 73.7 %psum.49 = f32[256]{0:T(256)S(1)} all-reduce(f32[256]{0:T(256)S(1)} %multiply_reduce_fusion.5), channel_id=1, replica_groups=mesh['rows'=32,'far'=8] {'rows'}, use_global_device_ids=true, to_apply=%region_1.0 | all-reduce | flops 256 | bytes 2048 | tf_op jit(solution)/shard_map/psum | solution.py:100
  87.7 2.9 copy.39
  90.7 4.3 gather_fusion.1
  95.0 6.5 fusion.18
  101.5 8.9 %all-to-all-start = ((f32[32,1,64,256]{3,2,1,0:T(8,128)}), f32[32,1,64,256]{3,2,1,0:T(8,128)}, u32[]{:S(2)}, u32[]{:S(2)}) async-start(f32[32,1,64,256]{3,2,1,0:T(8,128)} %fusion.18), calls=%async_computation | async-start | bytes 4194304 | tf_op jit(solution)/shard_map/all_to_all | solution.py:53
  110.4 3.1 fusion.49
  113.5 3.4 collective-permute-start
  116.9 3.8 collective-permute-start.1
  121.0 23.6 %collective-permute-done = f32[1024,256]{0,1:T(8,128)} collective-permute-done((f32[1024,256]{0,1:T(8,128)}, f32[1024,256]{0,1:T(8,128)}, u32[]{:S(2)}, u32[]{:S(2)}) %collective-permute-start) | collective-permute-done | bytes 1048608 | tf_op jit(solution)/shard_map/ppermute | solution.py:21
  144.6 2.2 collective-permute-done.1
  146.8 4.5 pad_maximum_fusion
  151.4 5.6 copy.37
  157.0 10.9 %gather_fusion = f32[96,128,256]{2,1,0:T(8,128)} fusion(f32[32,128,256]{2,1,0:T(8,128)} %bitcast.100, s32[1024]{0:T(1024)S(1)} %pad_clamp_fusion.1), kind=kCustom, calls=%fused_computation.clone | custom fusion | bytes 25166208 | tf_op jit(solution)/shard_map/jit(_take)/gather | solution.py:39
  167.9 10.1 %convolution_bitcast_fusion.1 = f32[32,128,256]{1,2,0:T(8,128)} fusion(f32[32,1,64,256]{3,2,1,0:T(8,128)} %all-to-all-done, f32[1,32,1,128,64]{3,4,2,1,0:T(8,128)S(1)} %copy-done), kind=kOutput, calls=%fused_computation.21 | convolution fusion | flops 805306368 | bytes 7340032 | tf_op jit(solution)/shard_map/asbr,asrn->asbn/dot_general | solution.py:50
  178.0 5.5 copy.41
  183.5 3.8 fusion.37
  187.3 21.8 %bitcast_add_fusion.1 = f32[16,128,256]{2,1,0:T(8,128)} fusion(f32[16,128,256]{2,0,1:T(8,128)S(1)} %fusion.37, f32[16,6,128,128]{3,2,1,0:T(8,128)} %param.12, f32[16,6,128,256]{3,2,1,0:T(8,128)} %bitcast.102, pred[16,6]{1,0:T(8,128)(4,1)S(1)} %copy.36), kind=kOutput, calls=%fused_computation.23 | convolution fusion | flops 4835508224 | bytes 23068768 | tf_op jit(solution)/shard_map/cspq,csqn->cpn/dot_general | solution.py:40
  209.1 2.9 copy.43
  212.0 89.7 %all-reduce.3.cloned.1.call-done = f32[2048,256]{0,1:T(8,128)} async-done(((f32[2048,256]{0,1:T(8,128)}), f32[2048,256]{0,1:T(8,128)}) %all-reduce.3.cloned.1.call-update) | async-done | bytes 2097168 | tf_op jit(solution)/shard_map/psum | solution.py:91
  301.7 3.3 multiply_add_fusion.1
  305.1 71.1 %psum.51 = f32[256]{0:T(256)S(1)} all-reduce(f32[256]{0:T(256)S(1)} %get-tuple-element.12), channel_id=1, replica_groups=mesh['rows'=32,'far'=8] {'rows'}, use_global_device_ids=true, to_apply=%region_4.7 | all-reduce | flops 256 | bytes 2048 | tf_op jit(solution)/shard_map/psum | solution.py:94
  376.2 2.2 multiply_reduce_fusion.3
  378.4 74.3 %psum.52 = f32[256]{0:T(256)S(1)} all-reduce(f32[256]{0:T(256)S(1)} %multiply_reduce_fusion.3), channel_id=1, replica_groups=mesh['rows'=32,'far'=8] {'rows'}, use_global_device_ids=true, to_apply=%region_6.9 | all-reduce | flops 256 | bytes 2048 | tf_op jit(solution)/shard_map/psum | solution.py:97
  452.7 3.5 broadcast_divide_fusion
  456.2 2.9 copy.47
  459.1 4.3 gather_fusion.3
  463.4 6.5 fusion.21
  469.9 5.9 all-to-all-start.1
  477.7 3.4 collective-permute-start.2
  481.1 2.5 collective-permute-start.3
  483.6 19.2 %collective-permute-done.2 = f32[1024,256]{0,1:T(8,128)S(1)} collective-permute-done((f32[1024,256]{0,1:T(8,128)S(1)}, f32[1024,256]{0,1:T(8,128)S(1)}, u32[]{:S(2)}, u32[]{:S(2)}) %collective-permute-start.2) | collective-permute-done | bytes 1048608 | tf_op jit(solution)/shard_map/ppermute | solution.py:21
  502.8 2.0 collective-permute-done.3
  504.9 2.2 pad_maximum_fusion.1
  507.1 5.8 copy.45
  512.9 10.9 %gather_fusion.2 = f32[96,128,256]{2,1,0:T(8,128)} fusion(f32[32,128,256]{2,1,0:T(8,128)} %bitcast.99, s32[1024]{0:T(1024)S(1)} %pad_clamp_fusion.1), kind=kCustom, calls=%fused_computation.2.clone | custom fusion | bytes 25166208 | tf_op jit(solution)/shard_map/jit(_take)/gather | solution.py:39
  523.8 10.1 %convolution_bitcast_fusion = f32[32,128,256]{1,2,0:T(8,128)} fusion(f32[32,1,64,256]{3,2,1,0:T(8,128)} %all-to-all-done.1, f32[1,32,1,128,64]{3,4,2,1,0:T(8,128)S(1)} %copy-done), kind=kOutput, calls=%fused_computation.20 | convolution fusion | flops 805306368 | bytes 7340032 | tf_op jit(solution)/shard_map/asbr,asrn->asbn/dot_general | solution.py:50
  533.9 5.5 copy.49
  539.4 3.8 fusion.35
  543.2 21.5 %bitcast_add_fusion = f32[16,128,256]{2,1,0:T(8,128)} fusion(f32[16,128,256]{2,0,1:T(8,128)S(1)} %fusion.35, f32[16,6,128,128]{3,2,1,0:T(8,128)} %param.12, f32[16,6,128,256]{3,2,1,0:T(8,128)} %bitcast.101, pred[16,6]{1,0:T(8,128)(4,1)S(1)} %copy.36), kind=kOutput, calls=%fused_computation.22 | convolution fusion | flops 4835508224 | bytes 23068768 | tf_op jit(solution)/shard_map/cspq,csqn->cpn/dot_general | solution.py:40
  564.7 2.9 copy.51
  567.6 82.0 %all-reduce.5.cloned.1.call-done = f32[2048,256]{0,1:T(8,128)} async-done(((f32[2048,256]{0,1:T(8,128)}), f32[2048,256]{0,1:T(8,128)}) %all-reduce.5.cloned.1.call-update) | async-done | bytes 2097168 | tf_op jit(solution)/shard_map/psum | solution.py:91
  649.6 4.0 multiply_reduce_fusion.2
  653.6 71.1 %psum.54 = f32[2,256]{1,0:T(2,128)S(1)} all-reduce(f32[2,256]{1,0:T(2,128)S(1)} %pad_maximum_fusion.2), channel_id=1, replica_groups=mesh['rows'=32,'far'=8] {'rows'}, use_global_device_ids=true, to_apply=%region_10.13 | all-reduce | flops 512 | bytes 4096 | tf_op jit(solution)/shard_map/psum | solution.py:94
  724.7 2.8 multiply_reduce_fusion
  727.6 74.1 %psum.55 = f32[256]{0:T(256)S(1)} all-reduce(f32[256]{0:T(256)S(1)} %multiply_reduce_fusion), channel_id=1, replica_groups=mesh['rows'=32,'far'=8] {'rows'}, use_global_device_ids=true, to_apply=%region_12.15 | all-reduce | flops 256 | bytes 2048 | tf_op jit(solution)/shard_map/psum | solution.py:97
  801.9 2.1 fusion.32
  (31 shorter events, 5.5 us)
Async XLA Ops:
  7.2 160.8 %copy-start = (f32[1,32,1,128,64]{3,4,2,1,0:T(8,128)S(1)}, f32[1,32,1,128,64]{3,4,2,1,0:T(8,128)}, u32[]{:S(2)}) copy-start(f32[1,32,1,128,64]{3,4,2,1,0:T(8,128)} %param.16) | copy-start | bytes 3145732
  101.5 66.4 %all-to-all-start = ((f32[32,1,64,256]{3,2,1,0:T(8,128)}), f32[32,1,64,256]{3,2,1,0:T(8,128)}, u32[]{:S(2)}, u32[]{:S(2)}) async-start(f32[32,1,64,256]{3,2,1,0:T(8,128)} %fusion.18), calls=%async_computation | async-start | bytes 4194304 | tf_op jit(solution)/shard_map/all_to_all | solution.py:53
  110.3 10.4 %copy-start.2 = (s32[16,6]{0,1:T(8,128)S(1)}, s32[16,6]{0,1:T(8,128)}, u32[]{:S(2)}) copy-start(s32[16,6]{0,1:T(8,128)} %param.13) | copy-start | bytes 1156
  110.3 191.4 %all-reduce.3.cloned.1.call-start = ((), (), s32[]{:S(2)}) async-start(), calls=%async_computation.2 | async-start | bytes 4194304 | tf_op jit(solution)/shard_map/psum | solution.py:91
  113.5 31.1 %collective-permute-start = (f32[1024,256]{0,1:T(8,128)}, f32[1024,256]{0,1:T(8,128)}, u32[]{:S(2)}, u32[]{:S(2)}) collective-permute-start(f32[1024,256]{0,1:T(8,128)} %get-tuple-element.15), channel_id=1, source_target_pairs={{0,8},{8,16},{16,24},{24,32},{32,40},{40,48},{48,56},{56,64},{64,7... | collective-permute-start | bytes 3145736 | tf_op jit(solution)/shard_map/ppermute | solution.py:21
  116.9 29.9 %collective-permute-start.1 = (f32[1024,256]{0,1:T(8,128)}, f32[1024,256]{0,1:T(8,128)}, u32[]{:S(2)}, u32[]{:S(2)}) collective-permute-start(f32[1024,256]{0,1:T(8,128)} %get-tuple-element.16), channel_id=1, source_target_pairs={{8,0},{16,8},{24,16},{32,24},{40,32},{48,40},{56,48},{64,56},{72,6... | collective-permute-start | bytes 3145736 | tf_op jit(solution)/shard_map/ppermute | solution.py:23
  178.0 5.5 copy-start.3
  469.9 53.9 %all-to-all-start.1 = ((f32[32,1,64,256]{3,2,1,0:T(8,128)}), f32[32,1,64,256]{3,2,1,0:T(8,128)}, u32[]{:S(2)}, u32[]{:S(2)}) async-start(f32[32,1,64,256]{3,2,1,0:T(8,128)} %fusion.21), calls=%async_computation.1 | async-start | bytes 4194304 | tf_op jit(solution)/shard_map/all_to_all | solution.py:53
  475.8 173.8 %all-reduce.5.cloned.1.call-start = ((), (), s32[]{:S(2)}) async-start(), calls=%async_computation.3 | async-start | bytes 4194304 | tf_op jit(solution)/shard_map/psum | solution.py:91
  475.9 29.0 %copy-start.1 = (f32[2048,256]{0,1:T(8,128)S(1)}, f32[2048,256]{0,1:T(8,128)}, u32[]{:S(2)}) copy-start(f32[2048,256]{0,1:T(8,128)} %broadcast_divide_fusion) | copy-start | bytes 6291460
  477.7 25.1 %collective-permute-start.2 = (f32[1024,256]{0,1:T(8,128)S(1)}, f32[1024,256]{0,1:T(8,128)S(1)}, u32[]{:S(2)}, u32[]{:S(2)}) collective-permute-start(f32[1024,256]{0,1:T(8,128)S(1)} %get-tuple-element.13), channel_id=1, source_target_pairs={{0,8},{8,16},{16,24},{24,32},{32,40},{40,48},{48,56},{56,64},{64,7... | collective-permute-start | bytes 3145736 | tf_op jit(solution)/shard_map/ppermute | solution.py:21
  481.1 23.8 %collective-permute-start.3 = (f32[1024,256]{0,1:T(8,128)S(1)}, f32[1024,256]{0,1:T(8,128)S(1)}, u32[]{:S(2)}, u32[]{:S(2)}) collective-permute-start(f32[1024,256]{0,1:T(8,128)S(1)} %get-tuple-element.14), channel_id=1, source_target_pairs={{8,0},{16,8},{24,16},{32,24},{40,32},{48,40},{56,48},{64,56},{72,6... | collective-permute-start | bytes 3145736 | tf_op jit(solution)/shard_map/ppermute | solution.py:23
Sparse Core Ops, SparseCore 0:
  212.1 89.5 all-reduce.2
  567.8 81.8 all-reduce.4
where the time goes:
time: 817 us; the launch traced here: 811 us
  blocking collectives  364 us (45%)
  waiting for transfers between devices  219 us (27%)
  matrix products  84 us (10%)
  local copies, waits for them, and re-layouts  71.9 us (9%)
  other arithmetic  29.8 us (4%)
  starting transfers between devices  27.9 us (3%)
  between operations  14.5 us (2%)
    psum x2, waiting for transfers between devices, apply_op(): return 0.5 * vector_in + lax.psum(partial_image(vector_in), 'far')  172 us
    psum x2, blocking collectives, orthogonal(): length = jnp.sqrt(lax.psum(column_dots(candidate, candidate), 'rows') + EPS)  148 us
    psum x2, blocking collectives, orthogonal(): lax.psum(jnp.stack([column_dots(item, candidate) for item in vectors]), '...  142 us
    psum x1, blocking collectives, shards(): lax.psum(column_dots(right_side, right_side), 'rows') + EPS  73.7 us
    dot_general x2, matrix products, near_term(): jnp.einsum('cspq,csqn->cpn', near_blocks, picked, precision=TOP_PRECISION)  43.3 us
    ppermute x2, waiting for transfers between devices, with_halo(): lax.ppermute(tail, axis, [(i, (i + 1) % count) for i in range(ends)])  42.8 us
    gather x2, local copies, waits for them, and re-layouts, near_term(): picked = jnp.take(clusters, near_cols - offset, axis=0)  21.8 us
    dot_general x2, matrix products, far_term(): jnp.einsum('asbr,asrn->asbn', far_left[0], lax.all_to_all(coefficients, '...  20.1 us
  transfers between devices with their start and end apart: 8, of which 6 were waited for; matrix products, arithmetic and copies ran while one was open for 6% of the time, Pallas kernels for 0%

commit v1 on v0

--- a/solution.py
+++ b/solution.py
@@ -97,7 +97,9 @@
         length = jnp.sqrt(lax.psum(column_dots(candidate, candidate), "rows") + EPS)
         return (heights, candidate, length)
 
-    rhs_length = jnp.sqrt(lax.psum(column_dots(right_side, right_side), "rows") + EPS)
+    rhs_length = jnp.sqrt(
+        jnp.sum(lax.all_gather(column_dots(right_side, right_side), "rows"), axis=0) + EPS
+    )
     first_full = right_side / rhs_length
     image_one = apply_op(first_full)
     heights_one, candidate, lower_left = orthogonal((first_full,), image_one)

time: 817 us -> 791 us (0.968)
  blocking collectives: 364 us -> 336 us
    psum x1 -> x0, blocking collectives: 73.7 us -> none  [shards(): lax.psum(column_dots(right_side, right_side), 'rows') + EPS]
    all_gather x0 -> x1, blocking collectives: none -> 45.5 us  [shards(): lax.all_gather(column_dots(right_side, right_side), 'rows')]
where the time goes in v1:
time: 791 us; the launch traced here: 785 us
  blocking collectives  336 us (42%)
  waiting for transfers between devices  223 us (28%)
  matrix products  83.9 us (11%)
  local copies, waits for them, and re-layouts  71.9 us (9%)
  other arithmetic  29.8 us (4%)
  starting transfers between devices  26 us (3%)
  between operations  14.5 us (2%)
    psum x2, waiting for transfers between devices, apply_op(): return 0.5 * vector_in + lax.psum(partial_image(vector_in), 'far')  172 us
    psum x2, blocking collectives, orthogonal(): length = jnp.sqrt(lax.psum(column_dots(candidate, candidate), 'rows') + EPS)  148 us
    psum x2, blocking collectives, orthogonal(): lax.psum(jnp.stack([column_dots(item, candidate) for item in vectors]), '...  142 us
    ppermute x2, waiting for transfers between devices, with_halo(): lax.ppermute(tail, axis, [(i, (i + 1) % count) for i in range(ends)])  47 us
    all_gather x1, blocking collectives, shards(): lax.all_gather(column_dots(right_side, right_side), 'rows')  45.5 us
    dot_general x2, matrix products, near_term(): jnp.einsum('cspq,csqn->cpn', near_blocks, picked, precision=TOP_PRECISION)  43.3 us
    gather x2, local copies, waits for them, and re-layouts, near_term(): picked = jnp.take(clusters, near_cols - offset, axis=0)  21.8 us
    dot_general x2, matrix products, far_term(): jnp.einsum('asbr,asrn->asbn', far_left[0], lax.all_to_all(coefficients, '...  20.1 us
  transfers between devices with their start and end apart: 8, of which 6 were waited for; matrix products, arithmetic and copies ran while one was open for 6% of the time, Pallas kernels for 0%

profile of v1, /device:TPU:2, one launch (start us, length us, event | category | flops | bytes accessed | tf_op | source)
XLA Modules:
  0.0 785.0 jit_solution(8211385906017657291)
XLA Ops:
  8.6 1.9 multiply_reduce_fusion.5
  10.5 1.9 copy.35
  12.4 45.5 %all-gather.1 = f32[32,1,256]{2,1,0:T(1,128)S(1)} all-gather(f32[1,1,256]{2,1,0:T(1,128)S(1)} %bitcast.112), channel_id=2, replica_groups=mesh['rows'=32,'far'=8] {'rows'}, dimensions={0}, use_global_device_ids=true | all-gather | bytes 33792 | tf_op jit(solution)/shard_map/all_gather | solution.py:101
  59.6 2.9 copy.39
  62.5 4.3 gather_fusion.1
  66.9 6.5 fusion.18
  73.3 7.0 all-to-all-start
  80.4 3.1 fusion.49
  83.5 3.4 collective-permute-start
  86.9 3.8 collective-permute-start.1
  91.0 27.8 %collective-permute-done = f32[1024,256]{0,1:T(8,128)} collective-permute-done((f32[1024,256]{0,1:T(8,128)}, f32[1024,256]{0,1:T(8,128)}, u32[]{:S(2)}, u32[]{:S(2)}) %collective-permute-start) | collective-permute-done | bytes 1048608 | tf_op jit(solution)/shard_map/ppermute | solution.py:21
  118.8 2.1 collective-permute-done.1
  120.9 4.5 pad_maximum_fusion
  125.4 5.6 copy.37
  131.0 10.9 %gather_fusion = f32[96,128,256]{2,1,0:T(8,128)} fusion(f32[32,128,256]{2,1,0:T(8,128)} %bitcast.101, s32[1024]{0:T(1024)S(1)} %pad_clamp_fusion.1), kind=kCustom, calls=%fused_computation.clone | custom fusion | bytes 25166208 | tf_op jit(solution)/shard_map/jit(_take)/gather | solution.py:39
  141.9 10.1 %convolution_bitcast_fusion.1 = f32[32,128,256]{1,2,0:T(8,128)} fusion(f32[32,1,64,256]{3,2,1,0:T(8,128)} %all-to-all-done, f32[1,32,1,128,64]{3,4,2,1,0:T(8,128)S(1)} %copy-done), kind=kOutput, calls=%fused_computation.21 | convolution fusion | flops 805306368 | bytes 7340032 | tf_op jit(solution)/shard_map/asbr,asrn->asbn/dot_general | solution.py:50
  152.0 5.5 copy.41
  157.5 3.8 fusion.37
  161.3 21.8 %bitcast_add_fusion.1 = f32[16,128,256]{2,1,0:T(8,128)} fusion(f32[16,128,256]{2,0,1:T(8,128)S(1)} %fusion.37, f32[16,6,128,128]{3,2,1,0:T(8,128)} %param.12, f32[16,6,128,256]{3,2,1,0:T(8,128)} %bitcast.103, pred[16,6]{1,0:T(8,128)(4,1)S(1)} %copy.36), kind=kOutput, calls=%fused_computation.23 | convolution fusion | flops 4835508224 | bytes 23068768 | tf_op jit(solution)/shard_map/cspq,csqn->cpn/dot_general | solution.py:40
  183.1 2.9 copy.43
  186.0 89.7 %all-reduce.3.cloned.1.call-done = f32[2048,256]{0,1:T(8,128)} async-done(((f32[2048,256]{0,1:T(8,128)}), f32[2048,256]{0,1:T(8,128)}) %all-reduce.3.cloned.1.call-update) | async-done | bytes 2097168 | tf_op jit(solution)/shard_map/psum | solution.py:91
  275.7 3.3 multiply_add_fusion.1
  279.0 71.1 %psum.43 = f32[256]{0:T(256)S(1)} all-reduce(f32[256]{0:T(256)S(1)} %get-tuple-element.12), channel_id=1, replica_groups=mesh['rows'=32,'far'=8] {'rows'}, use_global_device_ids=true, to_apply=%region_4.7 | all-reduce | flops 256 | bytes 2048 | tf_op jit(solution)/shard_map/psum | solution.py:94
  350.1 2.2 multiply_reduce_fusion.3
  352.3 74.3 %psum.44 = f32[256]{0:T(256)S(1)} all-reduce(f32[256]{0:T(256)S(1)} %multiply_reduce_fusion.3), channel_id=1, replica_groups=mesh['rows'=32,'far'=8] {'rows'}, use_global_device_ids=true, to_apply=%region_6.9 | all-reduce | flops 256 | bytes 2048 | tf_op jit(solution)/shard_map/psum | solution.py:97
  426.6 3.5 broadcast_divide_fusion
  430.1 2.9 copy.47
  433.1 4.3 gather_fusion.3
  437.4 6.5 fusion.21
  443.9 5.9 all-to-all-start.1
  451.7 3.4 collective-permute-start.2
  455.1 2.5 collective-permute-start.3
  457.6 19.2 %collective-permute-done.2 = f32[1024,256]{0,1:T(8,128)S(1)} collective-permute-done((f32[1024,256]{0,1:T(8,128)S(1)}, f32[1024,256]{0,1:T(8,128)S(1)}, u32[]{:S(2)}, u32[]{:S(2)}) %collective-permute-start.2) | collective-permute-done | bytes 1048608 | tf_op jit(solution)/shard_map/ppermute | solution.py:21
  476.8 2.0 collective-permute-done.3
  478.8 2.2 pad_maximum_fusion.1
  481.1 5.8 copy.45
  486.9 10.9 %gather_fusion.2 = f32[96,128,256]{2,1,0:T(8,128)} fusion(f32[32,128,256]{2,1,0:T(8,128)} %bitcast.100, s32[1024]{0:T(1024)S(1)} %pad_clamp_fusion.1), kind=kCustom, calls=%fused_computation.2.clone | custom fusion | bytes 25166208 | tf_op jit(solution)/shard_map/jit(_take)/gather | solution.py:39
  497.8 10.1 %convolution_bitcast_fusion = f32[32,128,256]{1,2,0:T(8,128)} fusion(f32[32,1,64,256]{3,2,1,0:T(8,128)} %all-to-all-done.1, f32[1,32,1,128,64]{3,4,2,1,0:T(8,128)S(1)} %copy-done), kind=kOutput, calls=%fused_computation.20 | convolution fusion | flops 805306368 | bytes 7340032 | tf_op jit(solution)/shard_map/asbr,asrn->asbn/dot_general | solution.py:50
  507.9 5.5 copy.49
  513.3 3.8 fusion.35
  517.1 21.5 %bitcast_add_fusion = f32[16,128,256]{2,1,0:T(8,128)} fusion(f32[16,128,256]{2,0,1:T(8,128)S(1)} %fusion.35, f32[16,6,128,128]{3,2,1,0:T(8,128)} %param.12, f32[16,6,128,256]{3,2,1,0:T(8,128)} %bitcast.102, pred[16,6]{1,0:T(8,128)(4,1)S(1)} %copy.36), kind=kOutput, calls=%fused_computation.22 | convolution fusion | flops 4835508224 | bytes 23068768 | tf_op jit(solution)/shard_map/cspq,csqn->cpn/dot_general | solution.py:40
  538.6 2.9 copy.51
  541.6 82.0 %all-reduce.5.cloned.1.call-done = f32[2048,256]{0,1:T(8,128)} async-done(((f32[2048,256]{0,1:T(8,128)}), f32[2048,256]{0,1:T(8,128)}) %all-reduce.5.cloned.1.call-update) | async-done | bytes 2097168 | tf_op jit(solution)/shard_map/psum | solution.py:91
  623.6 4.0 multiply_reduce_fusion.2
  627.5 71.1 %psum.46 = f32[2,256]{1,0:T(2,128)S(1)} all-reduce(f32[2,256]{1,0:T(2,128)S(1)} %pad_maximum_fusion.2), channel_id=1, replica_groups=mesh['rows'=32,'far'=8] {'rows'}, use_global_device_ids=true, to_apply=%region_10.13 | all-reduce | flops 512 | bytes 4096 | tf_op jit(solution)/shard_map/psum | solution.py:94
  698.7 2.8 multiply_reduce_fusion
  701.5 74.1 %psum.47 = f32[256]{0:T(256)S(1)} all-reduce(f32[256]{0:T(256)S(1)} %multiply_reduce_fusion), channel_id=1, replica_groups=mesh['rows'=32,'far'=8] {'rows'}, use_global_device_ids=true, to_apply=%region_12.15 | all-reduce | flops 256 | bytes 2048 | tf_op jit(solution)/shard_map/psum | solution.py:97
  775.8 2.1 fusion.32
  (32 shorter events, 5.6 us)
Async XLA Ops:
  7.2 134.8 %copy-start = (f32[1,32,1,128,64]{3,4,2,1,0:T(8,128)S(1)}, f32[1,32,1,128,64]{3,4,2,1,0:T(8,128)}, u32[]{:S(2)}) copy-start(f32[1,32,1,128,64]{3,4,2,1,0:T(8,128)} %param.16) | copy-start | bytes 3145732
  73.3 68.6 %all-to-all-start = ((f32[32,1,64,256]{3,2,1,0:T(8,128)}), f32[32,1,64,256]{3,2,1,0:T(8,128)}, u32[]{:S(2)}, u32[]{:S(2)}) async-start(f32[32,1,64,256]{3,2,1,0:T(8,128)} %fusion.18), calls=%async_computation | async-start | bytes 4194304 | tf_op jit(solution)/shard_map/all_to_all | solution.py:53
  80.3 10.4 %copy-start.2 = (s32[16,6]{0,1:T(8,128)S(1)}, s32[16,6]{0,1:T(8,128)}, u32[]{:S(2)}) copy-start(s32[16,6]{0,1:T(8,128)} %param.13) | copy-start | bytes 1156
  80.3 195.3 %all-reduce.3.cloned.1.call-start = ((), (), s32[]{:S(2)}) async-start(), calls=%async_computation.2 | async-start | bytes 4194304 | tf_op jit(solution)/shard_map/psum | solution.py:91
  83.5 35.3 %collective-permute-start = (f32[1024,256]{0,1:T(8,128)}, f32[1024,256]{0,1:T(8,128)}, u32[]{:S(2)}, u32[]{:S(2)}) collective-permute-start(f32[1024,256]{0,1:T(8,128)} %get-tuple-element.15), channel_id=1, source_target_pairs={{0,8},{8,16},{16,24},{24,32},{32,40},{40,48},{48,56},{56,64},{64,7... | collective-permute-start | bytes 3145736 | tf_op jit(solution)/shard_map/ppermute | solution.py:21
  86.9 34.0 %collective-permute-start.1 = (f32[1024,256]{0,1:T(8,128)}, f32[1024,256]{0,1:T(8,128)}, u32[]{:S(2)}, u32[]{:S(2)}) collective-permute-start(f32[1024,256]{0,1:T(8,128)} %get-tuple-element.16), channel_id=1, source_target_pairs={{8,0},{16,8},{24,16},{32,24},{40,32},{48,40},{56,48},{64,56},{72,6... | collective-permute-start | bytes 3145736 | tf_op jit(solution)/shard_map/ppermute | solution.py:23
  152.0 5.5 copy-start.3
  443.9 53.9 %all-to-all-start.1 = ((f32[32,1,64,256]{3,2,1,0:T(8,128)}), f32[32,1,64,256]{3,2,1,0:T(8,128)}, u32[]{:S(2)}, u32[]{:S(2)}) async-start(f32[32,1,64,256]{3,2,1,0:T(8,128)} %fusion.21), calls=%async_computation.1 | async-start | bytes 4194304 | tf_op jit(solution)/shard_map/all_to_all | solution.py:53
  449.8 173.8 %all-reduce.5.cloned.1.call-start = ((), (), s32[]{:S(2)}) async-start(), calls=%async_computation.3 | async-start | bytes 4194304 | tf_op jit(solution)/shard_map/psum | solution.py:91
  449.9 29.0 %copy-start.1 = (f32[2048,256]{0,1:T(8,128)S(1)}, f32[2048,256]{0,1:T(8,128)}, u32[]{:S(2)}) copy-start(f32[2048,256]{0,1:T(8,128)} %broadcast_divide_fusion) | copy-start | bytes 6291460
  451.7 25.1 %collective-permute-start.2 = (f32[1024,256]{0,1:T(8,128)S(1)}, f32[1024,256]{0,1:T(8,128)S(1)}, u32[]{:S(2)}, u32[]{:S(2)}) collective-permute-start(f32[1024,256]{0,1:T(8,128)S(1)} %get-tuple-element.13), channel_id=1, source_target_pairs={{0,8},{8,16},{16,24},{24,32},{32,40},{40,48},{48,56},{56,64},{64,7... | collective-permute-start | bytes 3145736 | tf_op jit(solution)/shard_map/ppermute | solution.py:21
  455.1 23.8 %collective-permute-start.3 = (f32[1024,256]{0,1:T(8,128)S(1)}, f32[1024,256]{0,1:T(8,128)S(1)}, u32[]{:S(2)}, u32[]{:S(2)}) collective-permute-start(f32[1024,256]{0,1:T(8,128)S(1)} %get-tuple-element.14), channel_id=1, source_target_pairs={{8,0},{16,8},{24,16},{32,24},{40,32},{48,40},{56,48},{64,56},{72,6... | collective-permute-start | bytes 3145736 | tf_op jit(solution)/shard_map/ppermute | solution.py:23
Sparse Core Ops, SparseCore 0:
  186.1 89.4 all-reduce.2
  541.7 81.7 all-reduce.4
